TPU v7x, 512 devices: a whole 4x8x8 slice. The times are simulated.
512 devices in a mesh: dp: 64 (over x, y, core), tensor: 8 (over z).
Axes of the slice: x: 4, y: 8, z: 8, core: 2. Of those that a mesh axis runs over, the one named last changes fastest.
Arguments:
- features: bfloat16 [65536, 4096], P(('dp', 'tensor')), may hold values from -20 to 20
- key_grads: bfloat16 [65536, 1024], P('dp', 'tensor'), may hold values from -20 to 20
- error_in: bfloat16 [64, 4096, 1024], P('dp', None, 'tensor'), may hold values from -24 to 24
- selected: int32 [64, 8, 128], P('dp', 'tensor'), may hold values from 0 to 4095, as said below
- bin_edges: int32 [17], replicated, may hold values from 0 to 4096, as said below
- threshold: int32 [1], replicated, may hold values from 1 to 15
- moment: float32 [4096, 1024], P('dp', 'tensor'), may hold values from -2 to 2
- second: float32 [4096, 1024], P('dp', 'tensor'), may hold values from 0.05 to 2
- master: float32 [4096, 1024], P('dp', 'tensor'), may hold values from -0.0625 to 0.0625
Outputs:
- keys: bfloat16 [65536, 1024], P('dp', 'tensor')
- error_out: bfloat16 [64, 4096, 1024], P('dp', None, 'tensor')
- moment_new: float32 [4096, 1024], P('dp', 'tensor')
- second_new: float32 [4096, 1024], P('dp', 'tensor')
- master_new: float32 [4096, 1024], P('dp', 'tensor')
Inputs may be any that keep to these rules, and one draw needn't show every extreme that they name: Each device's 128 rows are distinct; the rows o * 64 to (o + 1) * 64 - 1 form owner o's region, and one device's row of selected names at most 6 rows of one region; there is one region, the same for every row of selected, that receives exactly 6 blocks from each row; every other region receives at most 6 from a row. bin_edges[0] = 0, bin_edges[16] = 4096, strictly increasing.
All inputs are finite; a program needn't handle non-finite values.
Results may differ from a plain program's by a relative error of at most 0.001.
The roundings to bfloat16 on the way count: a program that leaves them out, or rounds other values in their place, can miss the bound.
Values may be sent and summed in bfloat16 or wider, within the bound.
A program may use at most 64 MiB of HBM per device.

v0:
```python
import math
import jax
import jax.numpy as jnp
from jax import lax
from jax.sharding import PartitionSpec as P

CAP = 6
beta_first = 0.9
beta_second = 0.95
learn_rate = 0.001
decay_rate = 0.1
epsilon = 1e-06
adam_epsilon = 1e-08
step_count = 10.0


def copy_for_each(value, axis):
    devices = lax.axis_size(axis)
    return lax.all_to_all(
        jnp.broadcast_to(value[None], (devices, *value.shape)), axis, 0, 0, tiled=True
    )


def over_copies(value, axis):
    everything = copy_for_each(value, axis)
    return jnp.sum(everything, axis=0)


def in_one_piece(arrays, axis, split_dim, concat_dim, along):
    widths = [math.prod(a.shape[along:]) for a in arrays]
    both = jnp.concatenate(
        [a.reshape(*a.shape[:along], w) for a, w in zip(arrays, widths)], axis=along
    )
    filled = lax.all_to_all(both, axis, split_axis=split_dim, concat_axis=concat_dim, tiled=True)
    blocks = jnp.split(filled, [sum(widths[:k]) for k in range(1, len(widths))], axis=along)
    return tuple(
        (b.reshape(*filled.shape[:along], *a.shape[along:]) for a, b in zip(arrays, blocks))
    )


def in_order(blocks, dim):
    dims = list(blocks.shape[1:])
    dims[dim] *= blocks.shape[0]
    return jnp.moveaxis(blocks, 0, dim).reshape(dims)


def gather_directly(value, axis, dim):
    return in_order(copy_for_each(value, axis), dim)


def shards(features, key_grads, error_in, selected, bin_edges, threshold, moment, second, master):
    highest = lax.Precision.HIGHEST
    whole = lax.all_gather(features, "tensor", axis=0, tiled=True)
    summed = lax.dot_general(
        whole, key_grads, (((0,), (0,)), ((), ())), preferred_element_type=jnp.float32
    )
    summed = summed + error_in[0].astype(jnp.float32)
    row_total = summed.shape[0]
    width_head = summed.shape[1]
    owners = lax.axis_size("dp")
    region = row_total // owners
    squares = jnp.sum(summed * summed, axis=1)
    row_ids = lax.iota(jnp.int32, row_total)
    member = (
        (row_ids[:, None] >= bin_edges[None, :-1]) & (row_ids[:, None] < bin_edges[None, 1:])
    ).astype(jnp.float32)
    energy = over_copies(jnp.dot(squares, member, precision=highest), "dp")
    widths = (bin_edges[1:] - bin_edges[:-1]).astype(jnp.float32)
    levels = lax.iota(jnp.int32, widths.shape[0])
    normal = 1.0 / jnp.sqrt(energy / (owners * width_head * widths) + epsilon)
    scale = jnp.where(levels >= threshold[0], normal, jnp.ones_like(normal))
    row_scale = jnp.dot(member, scale, precision=highest)
    chosen_ids = selected[0, 0]
    chosen = jnp.zeros((row_total,), jnp.float32).at[chosen_ids].set(1.0)
    kept = summed * chosen[:, None]
    error_out = (summed - kept).astype(jnp.bfloat16)[None]
    scaled = kept * row_scale[:, None]
    owner_of = chosen_ids // region
    owner_hot = (owner_of[:, None] == lax.iota(jnp.int32, owners)[None, :]).astype(jnp.int32)
    earlier = jnp.cumsum(owner_hot, axis=0) - owner_hot
    rank = jnp.sum(earlier * owner_hot, axis=1)
    slot = owner_of * CAP + rank
    outgoing = jnp.zeros((owners * CAP, width_head), jnp.float32).at[slot].set(scaled[chosen_ids])
    offsets = (
        jnp.full((owners * CAP,), region, jnp.float32)
        .at[slot]
        .set((chosen_ids % region).astype(jnp.float32))
    )
    arrived, places = in_one_piece(
        (outgoing.reshape(owners, CAP, width_head), offsets.reshape(owners, CAP)), "dp", 0, 0, 2
    )
    place_hot = (places.reshape(-1)[:, None] == lax.iota(jnp.float32, region)[None, :]).astype(
        jnp.float32
    )
    grad = lax.dot_general(
        place_hot, arrived.reshape(-1, width_head), (((0,), (0,)), ((), ())), precision=highest
    )
    moment_new = beta_first * moment + (1.0 - beta_first) * grad
    second_new = beta_second * second + (1.0 - beta_second) * grad * grad
    first_hat = moment_new / (1.0 - beta_first**step_count)
    second_hat = second_new / (1.0 - beta_second**step_count)
    master_new = master - learn_rate * (
        first_hat / (jnp.sqrt(second_hat) + adam_epsilon) + decay_rate * master
    )
    weight = master_new.astype(jnp.bfloat16)
    keys = jnp.dot(whole, gather_directly(weight, "dp", 0), preferred_element_type=jnp.float32)
    return (keys.astype(jnp.bfloat16), error_out, moment_new, second_new, master_new)


def solution(mesh):
    in_specs = (
        P(("dp", "tensor"), None),
        P("dp", "tensor"),
        P("dp", None, "tensor"),
        P("dp", "tensor", None),
        P(),
        P(),
        P("dp", "tensor"),
        P("dp", "tensor"),
        P("dp", "tensor"),
    )
    out_specs = (
        P("dp", "tensor"),
        P("dp", None, "tensor"),
        P("dp", "tensor"),
        P("dp", "tensor"),
        P("dp", "tensor"),
    )
    return jax.shard_map(shards, mesh=mesh, in_specs=in_specs, out_specs=out_specs, check_vma=False)
```

profile of v0, /device:TPU:1, one launch (start us, length us, event | category | flops | bytes accessed | tf_op | source)
XLA Modules:
  0.0 216.0 jit_solution(11072930889191832977)
XLA Ops:
  7.2 0.7 all-gather.2.cloned.1.call-update
  7.9 1.5 copy.28
  9.5 0.2 reduce_window_sum.11
  9.7 0.2 select_reduce_fusion
  10.0 103.0 %all-gather.2.cloned.1.call-done = bf16[1024,4096]{1,0:T(8,128)(2,1)} async-done(((bf16[128,4096]{1,0:T(8,128)(2,1)}), bf16[1024,4096]{1,0:T(8,128)(2,1)}) %all-gather.2.cloned.1.call-update) | async-done | bytes 8388624 | tf_op jit(solution)/shard_map/all_gather | solution.py:53
  112.9 4.9 %multiply_reduce_fusion = (f32[4096]{0:T(1024)S(1)}, f32[4096,128]{0,1:T(8,128)S(1)}) fusion(bf16[1,4096,128]{1,2,0:T(8,128)(2,1)S(1)} %copy.28, bf16[1024,4096]{1,0:T(8,128)(2,1)} %all-gather.2.cloned.1.call-done, bf16[1024,128]{1,0:T(8,128)(2,1)S(1)} %copy-done), kind=kOutput, calls=%fused_computation.8 | convolution fusion | flops 1075834880 | bytes 11812864 | tf_op jit(solution)/shard_map/dot_general | solution.py:54
  117.8 0.3 convolution_bitcast_fusion
  118.2 0.7 broadcast_in_dim.17
  118.8 10.5 %all-to-all-start = ((f32[64,1,16]{2,1,0:T(1,128)}), f32[64,1,16]{2,1,0:T(1,128)S(1)}, u32[]{:S(2)}, u32[]{:S(2)}) async-start(f32[64,1,16]{2,1,0:T(1,128)} %broadcast_in_dim.17), calls=%async_computation | async-start | bytes 65536 | tf_op jit(solution)/shard_map/all_to_all | solution.py:19
  130.1 1.0 scatter_custom_fusion.2
  131.0 0.9 reshape_reshape.4
  132.0 1.0 scatter_custom_fusion
  133.0 5.7 %all-to-all-done = f32[64,1,16]{2,1,0:T(1,128)S(1)} async-done(((f32[64,1,16]{2,1,0:T(1,128)}), f32[64,1,16]{2,1,0:T(1,128)S(1)}, u32[]{:S(2)}, u32[]{:S(2)}) %all-to-all-start) | async-done | bytes 4128 | tf_op jit(solution)/shard_map/all_to_all | solution.py:19
  138.7 0.3 fusion.4
  139.0 1.7 fusion.2
  140.8 1.9 copy.30
  142.7 1.9 scatter_custom_fusion.1
  144.6 1.0 reshape.153
  145.5 1.0 pad_maximum_fusion
  146.6 0.5 reshape.204
  147.0 15.6 %all_to_all.16 = f32[64,1,774]{2,1,0:T(1,128)S(1)} all-to-all(f32[64,1,774]{2,1,0:T(1,128)S(1)} %reshape.204), channel_id=1, replica_groups=mesh['dp'=64,'tensor'=8] {'dp'}, dimensions={0} | all-to-all | bytes 396288 | tf_op jit(solution)/shard_map/all_to_all | solution.py:34
  162.6 0.5 broadcast.187
  163.1 1.2 reduce.3
  164.3 0.3 reshape.205
  164.6 0.1 slice_reduce_fusion
  164.9 1.1 fusion.39
  166.0 1.3 broadcast_in_dim.19
  167.3 6.2 %all-to-all-start.2 = ((bf16[64,64,128]{2,1,0:T(8,128)(2,1)}), bf16[64,64,128]{2,1,0:T(8,128)(2,1)S(1)}, u32[]{:S(2)}, u32[]{:S(2)}) async-start(bf16[64,64,128]{2,1,0:T(8,128)(2,1)} %broadcast_in_dim.19), calls=%async_computation.2 | async-start | bytes 2097152 | tf_op jit(solution)/shard_map/all_to_all | solution.py:19
  173.5 1.3 copy.33
  174.8 27.2 %all-to-all-done.2 = bf16[64,64,128]{2,1,0:T(8,128)(2,1)S(1)} async-done(((bf16[64,64,128]{2,1,0:T(8,128)(2,1)}), bf16[64,64,128]{2,1,0:T(8,128)(2,1)S(1)}, u32[]{:S(2)}, u32[]{:S(2)}) %all-to-all-start.2) | async-done | bytes 1048608 | tf_op jit(solution)/shard_map/all_to_all | solution.py:19
  202.0 6.3 %fusion.1 = bf16[1024,128]{0,1:T(8,128)(2,1)S(1)} fusion(bf16[4096,128]{1,0:T(8,128)(2,1)S(1)} %bitcast.57, bf16[1024,4096]{1,0:T(8,128)(2,1)} %all-gather.2.cloned.1.call-done), kind=kOutput, calls=%fused_computation.10 | convolution fusion | flops 1073872896 | bytes 9699328 | tf_op jit(solution)/shard_map/dot_general | solution.py:106
  208.3 0.8 copy.32
  (23 shorter events, 0.5 us)
Async XLA Ops:
  7.2 105.8 %copy-start = (bf16[1024,128]{1,0:T(8,128)(2,1)S(1)}, bf16[1024,128]{1,0:T(8,128)(2,1)}, u32[]{:S(2)}) copy-start(bf16[1024,128]{1,0:T(8,128)(2,1)} %param.10) | copy-start | bytes 786436
  7.2 2.2 %copy-start.5 = (s32[1,1,128]{2,1,0:T(1,128)S(1)}, s32[1,1,128]{2,1,0:T(1,128)}, u32[]{:S(2)}) copy-start(s32[1,1,128]{2,1,0:T(1,128)} %param.12) | copy-start | bytes 1540
  7.2 2.7 %copy-start.4 = (s32[17]{0:T(128)S(1)}, s32[17]{0:T(128)}, u32[]{:S(2)}) copy-start(s32[17]{0:T(128)} %param.13) | copy-start | bytes 208
  7.2 105.7 %all-gather.2.cloned.1.call-start = ((), (), s32[]{:S(2)}) async-start(), calls=%async_computation.3 | async-start | bytes 9437184 | tf_op jit(solution)/shard_map/all_gather | solution.py:53
  118.8 19.8 %all-to-all-start = ((f32[64,1,16]{2,1,0:T(1,128)}), f32[64,1,16]{2,1,0:T(1,128)S(1)}, u32[]{:S(2)}, u32[]{:S(2)}) async-start(f32[64,1,16]{2,1,0:T(1,128)} %broadcast_in_dim.17), calls=%async_computation | async-start | bytes 65536 | tf_op jit(solution)/shard_map/all_to_all | solution.py:19
  146.5 18.4 %copy-start.1 = (f32[64,128]{1,0:T(8,128)S(1)}, f32[64,128]{1,0:T(8,128)}, u32[]{:S(2)}) copy-start(f32[64,128]{1,0:T(8,128)} %param.17) | copy-start | bytes 98308
  146.5 18.4 %copy-start.2 = (f32[64,128]{1,0:T(8,128)S(1)}, f32[64,128]{1,0:T(8,128)}, u32[]{:S(2)}) copy-start(f32[64,128]{1,0:T(8,128)} %param.15) | copy-start | bytes 98308
  146.6 18.4 %copy-start.3 = (f32[64,128]{1,0:T(8,128)S(1)}, f32[64,128]{1,0:T(8,128)}, u32[]{:S(2)}) copy-start(f32[64,128]{1,0:T(8,128)} %param.16) | copy-start | bytes 98308
  167.3 34.7 %all-to-all-start.2 = ((bf16[64,64,128]{2,1,0:T(8,128)(2,1)}), bf16[64,64,128]{2,1,0:T(8,128)(2,1)S(1)}, u32[]{:S(2)}, u32[]{:S(2)}) async-start(bf16[64,64,128]{2,1,0:T(8,128)(2,1)} %broadcast_in_dim.19), calls=%async_computation.2 | async-start | bytes 2097152 | tf_op jit(solution)/shard_map/all_to_all | solution.py:19
Sparse Core Ops, SparseCore 0:
  10.1 102.8 all-gather.1
where the time goes:
time: 217 us; the launch traced here: 216 us
  waiting for transfers between devices  137 us (63%)
  starting transfers between devices  16.8 us (8%)
  blocking collectives  15.6 us (7%)
  local copies, waits for them, and re-layouts  14.9 us (7%)
  between operations  14.9 us (7%)
  matrix products  12.8 us (6%)
  other arithmetic  4.47 us (2%)
    all_gather x1, waiting for transfers between devices, shards(): whole = lax.all_gather(features, 'tensor', axis=0, tiled=True)  103 us
    all_to_all x2, waiting for transfers between devices, copy_for_each(): lax.all_to_all(jnp.broadcast_to(value[None], (devices, *value.shape)), ax...  32.9 us
    all_to_all x2, starting transfers between devices, copy_for_each(): lax.all_to_all(jnp.broadcast_to(value[None], (devices, *value.shape)), ax...  16.7 us
    all_to_all x1, blocking collectives, in_one_piece(): lax.all_to_all(both, axis, split_axis=split_dim, concat_axis=concat_dim,...  15.6 us
    dot_general x1, matrix products, shards(): jnp.dot(whole, gather_directly(weight, 'dp', 0), preferred_element_type=j...  6.29 us
    dot_general x1, matrix products, shards(): lax.dot_general(whole, key_grads, (((0,), (0,)), ((), ())), preferred_ele...  4.88 us
    unnamed x17, local copies, waits for them, and re-layouts  4.38 us
  transfers between devices with their start and end apart: 3, of which 3 were waited for; matrix products, arithmetic and copies ran while one was open for 3% of the time, Pallas kernels for 0%

commit v1 on v0

--- a/solution.py
+++ b/solution.py
@@ -12,6 +12,14 @@
 epsilon = 1e-06
 adam_epsilon = 1e-08
 step_count = 10.0
+
+
+def gather_by_exchange(value, axis, dim):
+    size = lax.axis_size(axis)
+    repeats = [size if d == dim else 1 for d in range(value.ndim)]
+    return lax.all_to_all(
+        jnp.tile(value, repeats), axis, split_axis=dim, concat_axis=dim, tiled=True
+    )
 
 
 def copy_for_each(value, axis):
@@ -50,7 +58,7 @@
 
 def shards(features, key_grads, error_in, selected, bin_edges, threshold, moment, second, master):
     highest = lax.Precision.HIGHEST
-    whole = lax.all_gather(features, "tensor", axis=0, tiled=True)
+    whole = gather_by_exchange(features, "tensor", 0)
     summed = lax.dot_general(
         whole, key_grads, (((0,), (0,)), ((), ())), preferred_element_type=jnp.float32
     )

time: 217 us -> 301 us (1.39)
  waiting for transfers between devices: 137 us -> 219 us
  between operations: 14.9 us -> 1.52 us
  starting transfers between devices: 16.8 us -> 27.8 us
  local copies, waits for them, and re-layouts: 14.9 us -> 19.6 us
    all_to_all x0 -> x1, waiting for transfers between devices: none -> 186 us  [gather_by_exchange(): lax.all_to_all(jnp.tile(value, repeats), axis, split_axis=dim, concat_axi...]
    all_gather x1 -> x0, waiting for transfers between devices: 103 us -> none  [shards(): whole = lax.all_gather(features, 'tensor', axis=0, tiled=True)]
    all_to_all x0 -> x1, starting transfers between devices: none -> 11 us  [gather_by_exchange(): lax.all_to_all(jnp.tile(value, repeats), axis, split_axis=dim, concat_axi...]
    another operation x0 -> x1, local copies, waits for them, and re-layouts: none -> 5.53 us  [gather_by_exchange(): jnp.tile(value, repeats)]
  transfers between devices with their start and end apart: 3 -> 3, of which waited for: 3 -> 3; matrix products, arithmetic and copies ran while one was open for 3% -> 2% of each run, Pallas kernels for 0% -> 0%
where the time goes in v1:
time: 301 us; the launch traced here: 300 us
  waiting for transfers between devices  219 us (73%)
  starting transfers between devices  27.8 us (9%)
  local copies, waits for them, and re-layouts  19.6 us (7%)
  blocking collectives  15.6 us (5%)
  matrix products  12.8 us (4%)
  other arithmetic  4.47 us (1%)
    all_to_all x1, waiting for transfers between devices, gather_by_exchange(): lax.all_to_all(jnp.tile(value, repeats), axis, split_axis=dim, concat_axi...  186 us
    all_to_all x2, waiting for transfers between devices, copy_for_each(): lax.all_to_all(jnp.broadcast_to(value[None], (devices, *value.shape)), ax...  32.9 us
    all_to_all x2, starting transfers between devices, copy_for_each(): lax.all_to_all(jnp.broadcast_to(value[None], (devices, *value.shape)), ax...  16.8 us
    all_to_all x1, blocking collectives, in_one_piece(): lax.all_to_all(both, axis, split_axis=split_dim, concat_axis=concat_dim,...  15.6 us
    all_to_all x1, starting transfers between devices, gather_by_exchange(): lax.all_to_all(jnp.tile(value, repeats), axis, split_axis=dim, concat_axi...  11 us
    dot_general x1, matrix products, shards(): jnp.dot(whole, gather_directly(weight, 'dp', 0), preferred_element_type=j...  6.28 us
  transfers between devices with their start and end apart: 3, of which 3 were waited for; matrix products, arithmetic and copies ran while one was open for 2% of the time, Pallas kernels for 0%

profile of v1, /device:TPU:1, one launch (start us, length us, event | category | flops | bytes accessed | tf_op | source)
XLA Modules:
  0.0 300.3 jit_solution(16659596157775822518)
XLA Ops:
  0.6 5.5 %tile.2 = bf16[8,128,4096]{2,1,0:T(8,128)(2,1)} broadcast(bf16[128,4096]{1,0:T(8,128)(2,1)} %param.9), dimensions={1,2} | broadcast | bytes 9437184 | tf_op jit(solution)/shard_map/tile | solution.py:21
  6.2 11.0 %all-to-all-start = ((bf16[8,128,4096]{2,1,0:T(8,128)(2,1)}), bf16[8,128,4096]{2,1,0:T(8,128)(2,1)}, u32[]{:S(2)}, u32[]{:S(2)}) async-start(bf16[8,128,4096]{2,1,0:T(8,128)(2,1)} %tile.2), calls=%async_computation | async-start | bytes 16777216 | tf_op jit(solution)/shard_map/all_to_all | solution.py:20
  17.2 0.5 copy.28
  17.9 0.2 reduce_window_sum.11
  18.1 0.2 select_reduce_fusion
  18.4 185.7 %all-to-all-done = bf16[8,128,4096]{2,1,0:T(8,128)(2,1)} async-done(((bf16[8,128,4096]{2,1,0:T(8,128)(2,1)}), bf16[8,128,4096]{2,1,0:T(8,128)(2,1)}, u32[]{:S(2)}, u32[]{:S(2)}) %all-to-all-start) | async-done | bytes 8388640 | tf_op jit(solution)/shard_map/all_to_all | solution.py:20
  204.1 4.9 %multiply_reduce_fusion = (f32[4096]{0:T(1024)S(1)}, f32[4096,128]{0,1:T(8,128)S(1)}) fusion(bf16[1,4096,128]{1,2,0:T(8,128)(2,1)S(1)} %copy.28, bf16[1024,4096]{1,0:T(8,128)(2,1)} %bitcast.4, bf16[1024,128]{1,0:T(8,128)(2,1)S(1)} %copy-done), kind=kOutput, calls=%fused_computation.8 | convolution fusion | flops 1075834880 | bytes 11812864 | tf_op jit(solution)/shard_map/dot_general | solution.py:62
  208.9 0.3 convolution_bitcast_fusion
  209.3 0.7 broadcast_in_dim.17
  209.9 10.6 %all-to-all-start.1 = ((f32[64,1,16]{2,1,0:T(1,128)}), f32[64,1,16]{2,1,0:T(1,128)S(1)}, u32[]{:S(2)}, u32[]{:S(2)}) async-start(f32[64,1,16]{2,1,0:T(1,128)} %broadcast_in_dim.17), calls=%async_computation.1 | async-start | bytes 65536 | tf_op jit(solution)/shard_map/all_to_all | solution.py:27
  221.2 1.0 scatter_custom_fusion.2
  222.2 0.9 reshape_reshape.4
  223.1 1.0 scatter_custom_fusion
  224.1 5.7 %all-to-all-done.1 = f32[64,1,16]{2,1,0:T(1,128)S(1)} async-done(((f32[64,1,16]{2,1,0:T(1,128)}), f32[64,1,16]{2,1,0:T(1,128)S(1)}, u32[]{:S(2)}, u32[]{:S(2)}) %all-to-all-start.1) | async-done | bytes 4128 | tf_op jit(solution)/shard_map/all_to_all | solution.py:27
  229.9 0.3 fusion.4
  230.2 1.7 fusion.2
  231.9 1.9 copy.30
  233.8 1.9 scatter_custom_fusion.1
  235.7 1.0 reshape.160
  236.7 1.0 pad_maximum_fusion
  237.7 0.5 reshape.211
  238.2 15.6 %all_to_all.25 = f32[64,1,774]{2,1,0:T(1,128)S(1)} all-to-all(f32[64,1,774]{2,1,0:T(1,128)S(1)} %reshape.211), channel_id=1, replica_groups=mesh['dp'=64,'tensor'=8] {'dp'}, dimensions={0} | all-to-all | bytes 396288 | tf_op jit(solution)/shard_map/all_to_all | solution.py:42
  253.8 0.5 broadcast.190
  254.3 1.2 reduce.3
  255.5 0.3 reshape.212
  256.1 1.1 fusion.39
  257.1 1.3 broadcast_in_dim.19
  258.5 6.2 %all-to-all-start.3 = ((bf16[64,64,128]{2,1,0:T(8,128)(2,1)}), bf16[64,64,128]{2,1,0:T(8,128)(2,1)S(1)}, u32[]{:S(2)}, u32[]{:S(2)}) async-start(bf16[64,64,128]{2,1,0:T(8,128)(2,1)} %broadcast_in_dim.19), calls=%async_computation.3 | async-start | bytes 2097152 | tf_op jit(solution)/shard_map/all_to_all | solution.py:27
  264.7 1.3 copy.33
  266.0 27.2 %all-to-all-done.3 = bf16[64,64,128]{2,1,0:T(8,128)(2,1)S(1)} async-done(((bf16[64,64,128]{2,1,0:T(8,128)(2,1)}), bf16[64,64,128]{2,1,0:T(8,128)(2,1)S(1)}, u32[]{:S(2)}, u32[]{:S(2)}) %all-to-all-start.3) | async-done | bytes 1048608 | tf_op jit(solution)/shard_map/all_to_all | solution.py:27
  293.2 6.3 %fusion.1 = bf16[1024,128]{0,1:T(8,128)(2,1)S(1)} fusion(bf16[4096,128]{1,0:T(8,128)(2,1)S(1)} %bitcast.58, bf16[1024,4096]{1,0:T(8,128)(2,1)} %bitcast.4), kind=kOutput, calls=%fused_computation.10 | convolution fusion | flops 1073872896 | bytes 9699328 | tf_op jit(solution)/shard_map/dot_general | solution.py:114
  299.5 0.8 copy.32
  (25 shorter events, 0.7 us)
Async XLA Ops:
  0.6 203.4 %copy-start = (bf16[1024,128]{1,0:T(8,128)(2,1)S(1)}, bf16[1024,128]{1,0:T(8,128)(2,1)}, u32[]{:S(2)}) copy-start(bf16[1024,128]{1,0:T(8,128)(2,1)} %param.10) | copy-start | bytes 786436
  6.2 11.0 %copy-start.1 = (bf16[1,4096,128]{2,1,0:T(8,128)(2,1)S(1)}, bf16[1,4096,128]{2,1,0:T(8,128)(2,1)}, u32[]{:S(2)}) copy-start(bf16[1,4096,128]{2,1,0:T(8,128)(2,1)} %param.11) | copy-start | bytes 3145732
  6.2 197.9 %all-to-all-start = ((bf16[8,128,4096]{2,1,0:T(8,128)(2,1)}), bf16[8,128,4096]{2,1,0:T(8,128)(2,1)}, u32[]{:S(2)}, u32[]{:S(2)}) async-start(bf16[8,128,4096]{2,1,0:T(8,128)(2,1)} %tile.2), calls=%async_computation | async-start | bytes 16777216 | tf_op jit(solution)/shard_map/all_to_all | solution.py:20
  17.2 0.7 copy-start.6
  17.2 1.1 copy-start.5
  209.9 19.9 %all-to-all-start.1 = ((f32[64,1,16]{2,1,0:T(1,128)}), f32[64,1,16]{2,1,0:T(1,128)S(1)}, u32[]{:S(2)}, u32[]{:S(2)}) async-start(f32[64,1,16]{2,1,0:T(1,128)} %broadcast_in_dim.17), calls=%async_computation.1 | async-start | bytes 65536 | tf_op jit(solution)/shard_map/all_to_all | solution.py:27
  237.7 18.4 %copy-start.2 = (f32[64,128]{1,0:T(8,128)S(1)}, f32[64,128]{1,0:T(8,128)}, u32[]{:S(2)}) copy-start(f32[64,128]{1,0:T(8,128)} %param.17) | copy-start | bytes 98308
  237.7 18.4 %copy-start.3 = (f32[64,128]{1,0:T(8,128)S(1)}, f32[64,128]{1,0:T(8,128)}, u32[]{:S(2)}) copy-start(f32[64,128]{1,0:T(8,128)} %param.15) | copy-start | bytes 98308
  237.7 18.4 %copy-start.4 = (f32[64,128]{1,0:T(8,128)S(1)}, f32[64,128]{1,0:T(8,128)}, u32[]{:S(2)}) copy-start(f32[64,128]{1,0:T(8,128)} %param.16) | copy-start | bytes 98308
  258.5 34.7 %all-to-all-start.3 = ((bf16[64,64,128]{2,1,0:T(8,128)(2,1)}), bf16[64,64,128]{2,1,0:T(8,128)(2,1)S(1)}, u32[]{:S(2)}, u32[]{:S(2)}) async-start(bf16[64,64,128]{2,1,0:T(8,128)(2,1)} %broadcast_in_dim.19), calls=%async_computation.3 | async-start | bytes 2097152 | tf_op jit(solution)/shard_map/all_to_all | solution.py:27
